TPU v7x, 256 devices: a whole 4x4x8 slice. The times are simulated.
256 devices in a mesh: px: 4 (over z_lo), py: 8 (over y, core), ch: 8 (over z_hi, x).
Axes of the slice: x: 4, y: 4, z: 8 (z_hi: 2, z_lo: 4; z = z_hi * 4 + z_lo), core: 2. Of those that a mesh axis runs over, the one named last changes fastest.
Arguments:
- features: bfloat16 [128, 12, 8, 4, 512], P('ch', None, 'py', 'px'), may hold values from -6 to 6
- cotangent: bfloat16 [128, 12, 8, 4, 512], P('ch', None, 'py', 'px'), may hold values from -6 to 6
- weight: bfloat16 [3, 3, 128, 128], replicated, may hold values from -0.1875 to 0.1875
- edge_table: int32 [12, 4, 3], replicated, may hold values from 0 to 11, as said below
- corner_table: int32 [12, 4, 2], replicated, may hold values from 0 to 11, as said below
Outputs:
- activation: bfloat16 [128, 12, 8, 4, 512], P('ch', None, 'py', 'px')
- input_grad: bfloat16 [128, 12, 8, 4, 512], P('ch', None, 'py', 'px')
Inputs may be any that keep to these rules, and one draw needn't show every extreme that they name: edge_table[f, e] = (g, s, r): beyond edge e of face f lie the pixels of side s of face g, in reverse order if r = 1; every side of every face is named exactly once, and if (f, e) names (g, s) then (g, s) names (f, e) with the same r. corner_table[f, c] = (h, q): corner c of face f takes corner pixel q of face h; in each corner column every face appears once, and each q appears 12 times.
All inputs are finite; a program needn't handle non-finite values.
Results may differ from a plain program's by a relative error of at most 0.0049.
Values may be sent and summed in bfloat16 or wider, within the bound.
A program may use at most 192 MiB of HBM per device.

v0:
```python
import jax
import jax.numpy as jnp
from jax import lax
from jax.sharding import PartitionSpec as P

RB = 32


def with_halo(array, sides, width):
    for axis, dim in sides:
        size, length = (lax.axis_size(axis), array.shape[dim])
        up = [(i, (i + 1) % size) for i in range(size - 1)]
        down = [(j, i) for i, j in up]
        last = lax.slice_in_dim(array, length - width, length, axis=dim)
        leading = lax.slice_in_dim(array, 0, width, axis=dim)
        before = lax.ppermute(last, axis, up)
        after = lax.ppermute(leading, axis, down)
        array = jnp.concatenate([before, array, after], axis=dim)
    return array


def edge_strips(lines, edge_table, corner_table):
    chan_count = lines.shape[0]
    face_count = lines.shape[1]
    side_len = lines.shape[3]
    flat_lines = lines.reshape(chan_count, face_count * 4, side_len)
    pixels = jnp.stack(
        [lines[:, :, 0, 0], lines[:, :, 0, -1], lines[:, :, 1, 0], lines[:, :, 1, -1]], axis=2
    ).reshape(chan_count, face_count * 4)
    corner_index = corner_table[:, :, 0] * 4 + corner_table[:, :, 1]
    corner_vals = jnp.take(pixels, corner_index, axis=1)
    strips = []
    for edge_num, start_corner, end_corner in ((0, 0, 1), (1, 2, 3), (2, 0, 2), (3, 1, 3)):
        source_row = edge_table[:, edge_num, 0] * 4 + edge_table[:, edge_num, 1]
        strip_line = jnp.take(flat_lines, source_row, axis=1)
        flipped = (edge_table[:, edge_num, 2] == 1)[None, :, None]
        strip_line = jnp.where(flipped, strip_line[:, :, ::-1], strip_line)
        strips.append(
            jnp.concatenate(
                [
                    corner_vals[:, :, start_corner : start_corner + 1],
                    strip_line,
                    corner_vals[:, :, end_corner : end_corner + 1],
                ],
                axis=2,
            )
        )
    return strips


def face_lines_of(field, row_pos, col_pos, px_count, py_count):
    chan_block = field.shape[0]
    face_count = field.shape[1]
    col_len = field.shape[2]
    row_len = field.shape[3]
    side_len = row_len * px_count
    blank = jnp.zeros((chan_block, face_count, side_len), jnp.float32)

    def placed(values, offset, active):
        return jnp.where(
            active,
            lax.dynamic_update_slice_in_dim(blank, values.astype(jnp.float32), offset, 2),
            0.0,
        )

    contrib = jnp.stack(
        [
            placed(field[:, :, 0, :], row_pos * row_len, col_pos == 0),
            placed(field[:, :, -1, :], row_pos * row_len, col_pos == py_count - 1),
            placed(field[:, :, :, 0], col_pos * col_len, row_pos == 0),
            placed(field[:, :, :, -1], col_pos * col_len, row_pos == px_count - 1),
        ],
        axis=2,
    )
    return lax.psum(contrib.astype(jnp.bfloat16), ("px", "py"))


def pad_field(field, edge_table, corner_table):
    col_len = field.shape[2]
    row_len = field.shape[3]
    row_pos = lax.axis_index("px")
    col_pos = lax.axis_index("py")
    px_count = lax.axis_size("px")
    py_count = lax.axis_size("py")
    padded = with_halo(field, (("px", 3), ("py", 2)), 1)
    lines = face_lines_of(field, row_pos, col_pos, px_count, py_count)
    strips = edge_strips(lines, edge_table, corner_table)
    top_row = lax.dynamic_slice_in_dim(strips[0], row_pos * row_len, row_len + 2, 2)
    bottom_row = lax.dynamic_slice_in_dim(strips[1], row_pos * row_len, row_len + 2, 2)
    left_col = lax.dynamic_slice_in_dim(strips[2], col_pos * col_len, col_len + 2, 2)
    right_col = lax.dynamic_slice_in_dim(strips[3], col_pos * col_len, col_len + 2, 2)
    padded = padded.at[:, :, 0, :].set(jnp.where(col_pos == 0, top_row, padded[:, :, 0, :]))
    padded = padded.at[:, :, -1, :].set(
        jnp.where(col_pos == py_count - 1, bottom_row, padded[:, :, -1, :])
    )
    padded = padded.at[:, :, :, 0].set(jnp.where(row_pos == 0, left_col, padded[:, :, :, 0]))
    padded = padded.at[:, :, :, -1].set(
        jnp.where(row_pos == px_count - 1, right_col, padded[:, :, :, -1])
    )
    return padded


def forward_taps(padded, taps, out_cols, out_rows):
    summed = None
    for tap_row in range(3):
        for tap_col in range(3):
            window = padded[:, :, tap_row : tap_row + out_cols, tap_col : tap_col + out_rows]
            term_val = jnp.einsum(
                "oc,cfab->ofab", taps[tap_row, tap_col], window, preferred_element_type=jnp.float32
            )
            summed = term_val if summed is None else summed + term_val
    return summed


def backward_taps(padded, taps, out_cols, out_rows):
    summed = None
    for tap_row in range(3):
        for tap_col in range(3):
            window = padded[
                :, :, 2 - tap_row : 2 - tap_row + out_cols, 2 - tap_col : 2 - tap_col + out_rows
            ]
            term_val = jnp.einsum(
                "oc,ofab->cfab", taps[tap_row, tap_col], window, preferred_element_type=jnp.float32
            )
            summed = term_val if summed is None else summed + term_val
    return summed


def gate_outputs(preact, cotangent):
    sigmoid_val = jax.nn.sigmoid(preact)
    activation = (preact * sigmoid_val).astype(jnp.bfloat16)
    gated = (
        cotangent.astype(jnp.float32) * sigmoid_val * (1.0 + preact * (1.0 - sigmoid_val))
    ).astype(jnp.bfloat16)
    return (activation, gated)


def local(features, cotangent, weight, edge_table, corner_table):
    chan_block = features.shape[0]
    face_count = features.shape[1]
    tile_len = features.shape[4]
    row_len = RB
    col_len = tile_len // row_len
    features = features.reshape(chan_block, face_count, col_len, row_len)
    cotangent = cotangent.reshape(chan_block, face_count, col_len, row_len)
    ch_pos = lax.axis_index("ch")
    feat_pad = pad_field(features, edge_table, corner_table)
    own_taps = lax.dynamic_slice_in_dim(weight, ch_pos * chan_block, chan_block, 2)
    piece_taps = own_taps
    preact = forward_taps(
        lax.all_gather(feat_pad, "ch", axis=0, tiled=True), piece_taps, col_len, row_len
    )
    activation, gated = gate_outputs(preact, cotangent)
    grad_pad = pad_field(gated, edge_table, corner_table)
    input_taps = lax.dynamic_slice_in_dim(weight, ch_pos * chan_block, chan_block, 3)
    piece_taps = input_taps
    input_grad = backward_taps(
        lax.all_gather(grad_pad, "ch", axis=0, tiled=True), piece_taps, col_len, row_len
    ).astype(jnp.bfloat16)
    out_shape = (chan_block, face_count, 1, 1, tile_len)
    return (activation.reshape(out_shape), input_grad.reshape(out_shape))


def solution(mesh):
    return jax.shard_map(
        local,
        mesh=mesh,
        in_specs=(P("ch", None, "py", "px", None), P("ch", None, "py", "px", None), P(), P(), P()),
        out_specs=(P("ch", None, "py", "px", None), P("ch", None, "py", "px", None)),
        check_vma=False,
    )
```

profile of v0, /device:TPU:8, one launch (start us, length us, event | category | flops | bytes accessed | tf_op | source)
XLA Modules:
  0.0 1055.1 jit_solution(10775510683861696942)
XLA Ops:
  11.2 3.0 copy.696
  16.1 2.7 select_n.196
  18.7 2.7 select_n.200
  23.1 2.6 copy.698
  27.0 7.1 collective-permute-start
  43.6 1.9 collective-permute-start.2
  45.5 3.9 collective-permute-start.3
  53.1 254.8 %all-reduce.3.cloned.1.call-done = bf16[16,12,4,128]{1,0,3,2:T(8,128)(2,1)} async-done(((bf16[16,12,4,128]{1,0,3,2:T(8,128)(2,1)}), bf16[16,12,4,128]{1,0,3,2:T(8,128)(2,1)}) %all-reduce.3.cloned.1.call-update) | async-done | bytes 196624 | tf_op jit(solution)/shard_map/psum | solution.py:75
  307.9 3.0 copy.702
  318.9 3.8 scatter.30
  326.8 18.3 %scatter.31 = bf16[16,12,18,34]{3,0,2,1:T(8,128)(2,1)S(1)} dynamic-update-slice(bf16[16,12,18,34]{3,0,2,1:T(8,128)(2,1)S(1)} %scatter.30, bf16[16,12,18,1]{3,0,2,1:T(8,128)(2,1)S(1)} %copy.707, s32[]{:T(128)} %constant.235.clone.1, s32[]{:T(128)} %constant.235.clone.1, s32[]{:T(128)} %constant.235.clone.1, s32[]{:T(128)} %constant.249.clone.1) | dynamic-update-slice | bytes 13828 | tf_op jit(solution)/shard_map/scatter | solution.py:97
  347.9 162.8 %all-gather.3.cloned.1.call-done = bf16[128,12,18,34]{3,0,2,1:T(8,128)(2,1)} async-done(((bf16[16,12,18,34]{3,0,2,1:T(8,128)(2,1)}), bf16[128,12,18,34]{3,0,2,1:T(8,128)(2,1)}) %all-gather.3.cloned.1.call-update) | async-done | bytes 1880080 | tf_op jit(solution)/shard_map/all_gather | solution.py:151
  510.7 4.7 fusion.20
  524.6 2.0 fusion.18
  526.6 2.6 fusion.37
  531.6 2.3 copy.725
  536.3 2.2 collective-permute-start.4
  541.1 1.9 select_n.220
  543.0 1.9 select_n.223
  545.7 2.6 copy.727
  551.1 1.9 collective-permute-start.6
  553.0 3.9 collective-permute-start.7
  559.2 266.2 %all-reduce.5.cloned.1.call-done = bf16[16,12,4,128]{1,0,3,2:T(8,128)(2,1)} async-done(((bf16[16,12,4,128]{1,0,3,2:T(8,128)(2,1)}), bf16[16,12,4,128]{1,0,3,2:T(8,128)(2,1)}) %all-reduce.5.cloned.1.call-update) | async-done | bytes 196624 | tf_op jit(solution)/shard_map/psum | solution.py:75
  825.4 3.0 copy.731
  837.1 3.8 scatter.36
  844.2 18.6 %scatter.39 = bf16[16,12,18,34]{3,0,2,1:T(8,128)(2,1)S(1)} dynamic-update-slice(bf16[16,12,18,34]{3,0,2,1:T(8,128)(2,1)S(1)} %scatter.36, bf16[16,12,18,1]{3,0,2,1:T(8,128)(2,1)S(1)} %copy.735, s32[]{:T(128)} %constant.235.clone.1, s32[]{:T(128)} %constant.235.clone.1, s32[]{:T(128)} %constant.235.clone.1, s32[]{:T(128)} %constant.249.clone.1) | dynamic-update-slice | bytes 13828 | tf_op jit(solution)/shard_map/scatter | solution.py:97
  865.5 162.9 %all-gather.5.cloned.1.call-done = bf16[128,12,18,34]{3,0,2,1:T(8,128)(2,1)} async-done(((bf16[16,12,18,34]{3,0,2,1:T(8,128)(2,1)}), bf16[128,12,18,34]{3,0,2,1:T(8,128)(2,1)}) %all-gather.5.cloned.1.call-update) | async-done | bytes 1880080 | tf_op jit(solution)/shard_map/all_gather | solution.py:158
  1028.4 4.8 fusion.2
  1034.3 1.9 fusion.10
  1037.2 1.9 fusion.14
  1040.9 1.9 fusion.8
  1044.1 2.3 add_convert_fusion
  (201 shorter events, 80.0 us)
Async XLA Ops:
  7.2 503.6 %copy-start = (bf16[3,3,128,128]{3,2,1,0:T(8,128)(2,1)S(1)}, bf16[3,3,128,128]{3,2,1,0:T(8,128)(2,1)}, u32[]{:S(2)}) copy-start(bf16[3,3,128,128]{3,2,1,0:T(8,128)(2,1)} %param.27) | copy-start | bytes 884740
  7.2 300.8 %all-reduce.3.cloned.1.call-start = ((), (), s32[]{:S(2)}) async-start(), calls=%async_computation | async-start | bytes 4194304 | tf_op jit(solution)/shard_map/psum | solution.py:75
  25.7 10.9 %copy-start.17 = (s32[12,4,3]{0,1,2:T(4,128)S(1)}, s32[12,4,3]{0,1,2:T(4,128)}, u32[]{:S(2)}) copy-start(s32[12,4,3]{0,1,2:T(4,128)} %param.28) | copy-start | bytes 1732
  25.7 12.0 %copy-start.26 = (s32[12,4,2]{0,2,1:T(2,128)S(1)}, s32[12,4,2]{0,2,1:T(2,128)}, u32[]{:S(2)}) copy-start(s32[12,4,2]{0,2,1:T(2,128)} %param.29) | copy-start | bytes 1156
  25.7 485.0 %all-gather.3.cloned.1.call-start = ((), (), s32[]{:S(2)}) async-start(), calls=%async_computation.1 | async-start | bytes 7962624 | tf_op jit(solution)/shard_map/all_gather | solution.py:151
  27.0 12.3 %collective-permute-start = (bf16[16,12,16,1]{2,0,3,1:T(8,128)(2,1)S(1)}, bf16[16,12,16,1]{2,0,3,1:T(8,128)(2,1)S(1)}, u32[]{:S(2)}, u32[]{:S(2)}) collective-permute-start(bf16[16,12,16,1]{2,0,3,1:T(8,128)(2,1)S(1)} %copy.684), channel_id=1, source_target_pairs={{0,64},{64,128},{128,192},{1,65},{65,129},{129,193},{2,66},{66,130... | collective-permute-start | bytes 18440 | tf_op jit(solution)/shard_map/ppermute | solution.py:16
  35.3 6.0 collective-permute-start.1
  43.6 5.9 collective-permute-start.2
  45.5 5.4 collective-permute-start.3
  53.1 258.7 %copy-start.15 = (pred[12]{0:T(512)(128)(4,1)S(1)}, pred[12]{0:T(512)(128)(4,1)}, u32[]{:S(2)}) copy-start(pred[12]{0:T(512)(128)(4,1)} %get-tuple-element.166) | copy-start | bytes 40
  53.1 259.6 %copy-start.13 = (pred[12]{0:T(512)(128)(4,1)S(1)}, pred[12]{0:T(512)(128)(4,1)}, u32[]{:S(2)}) copy-start(pred[12]{0:T(512)(128)(4,1)} %get-tuple-element.164) | copy-start | bytes 40
  311.0 4.6 copy-start.20
  311.0 4.7 copy-start.11
  311.0 4.9 copy-start.22
  313.8 3.6 copy-start.24
  346.1 479.3 %all-reduce.5.cloned.1.call-start = ((), (), s32[]{:S(2)}) async-start(), calls=%async_computation.2 | async-start | bytes 4194304 | tf_op jit(solution)/shard_map/psum | solution.py:75
  510.7 4.8 copy-start.2
  535.1 9.9 copy-start.7
  535.1 10.2 copy-start.6
  536.3 12.1 %collective-permute-start.4 = (bf16[16,12,16,1]{2,0,3,1:T(8,128)(2,1)S(1)}, bf16[16,12,16,1]{2,0,3,1:T(8,128)(2,1)S(1)}, u32[]{:S(2)}, u32[]{:S(2)}) collective-permute-start(bf16[16,12,16,1]{2,0,3,1:T(8,128)(2,1)S(1)} %copy.720), channel_id=1, source_target_pairs={{0,64},{64,128},{128,192},{1,65},{65,129},{129,193},{2,66},{66,130... | collective-permute-start | bytes 18440 | tf_op jit(solution)/shard_map/ppermute | solution.py:16
  539.8 9.9 collective-permute-start.5
  548.4 480.1 %all-gather.5.cloned.1.call-start = ((), (), s32[]{:S(2)}) async-start(), calls=%async_computation.3 | async-start | bytes 7962624 | tf_op jit(solution)/shard_map/all_gather | solution.py:158
  551.1 5.8 collective-permute-start.6
  553.0 5.4 collective-permute-start.7
  559.1 272.2 %copy-start.16 = (pred[12]{0:T(512)(128)(4,1)S(1)}, pred[12]{0:T(512)(128)(4,1)}, u32[]{:S(2)}) copy-start(pred[12]{0:T(512)(128)(4,1)} %get-tuple-element.166) | copy-start | bytes 40
  559.2 272.4 %copy-start.25 = (pred[12]{0:T(512)(128)(4,1)S(1)}, pred[12]{0:T(512)(128)(4,1)}, u32[]{:S(2)}) copy-start(pred[12]{0:T(512)(128)(4,1)} %get-tuple-element.162) | copy-start | bytes 40
  559.2 272.5 %copy-start.14 = (pred[12]{0:T(512)(128)(4,1)S(1)}, pred[12]{0:T(512)(128)(4,1)}, u32[]{:S(2)}) copy-start(pred[12]{0:T(512)(128)(4,1)} %get-tuple-element.164) | copy-start | bytes 40
  559.2 272.7 %copy-start.23 = (pred[12]{0:T(512)(128)(4,1)S(1)}, pred[12]{0:T(512)(128)(4,1)}, u32[]{:S(2)}) copy-start(pred[12]{0:T(512)(128)(4,1)} %get-tuple-element.161) | copy-start | bytes 40
  828.4 5.5 copy-start.21
  828.5 5.6 copy-start.9
  842.9 20.9 %copy-start.5 = (bf16[16,12,16,32]{3,0,2,1:T(8,128)(2,1)S(1)}, bf16[16,12,16,32]{3,0,2,1:T(8,128)(2,1)}, u32[]{:S(2)}) copy-start(bf16[16,12,16,32]{3,0,2,1:T(8,128)(2,1)} %get-tuple-element.139) | copy-start | bytes 589828
  1028.4 4.8 copy-start.1
  (7 other events, 9.8 us)
Sparse Core Ops, SparseCore 0:
  25.8 282.0 all-reduce.2
  346.2 164.4 all-gather.2
  548.5 276.8 all-reduce.4
  863.9 164.4 all-gather.4
where the time goes:
time: 1060 us
  waiting for transfers between devices  850 us (80%)
  local copies, waits for them, and re-layouts  117 us (11%)
  matrix products  36.3 us (3%)
  starting transfers between devices  24 us (2%)
  between operations  15.2 us (1%)
  other arithmetic  12.9 us (1%)
    psum x2, waiting for transfers between devices, face_lines_of(): return lax.psum(contrib.astype(jnp.bfloat16), ('px', 'py'))  521 us
    all_gather x1, waiting for transfers between devices, local(): lax.all_gather(grad_pad, 'ch', axis=0, tiled=True)  163 us
    all_gather x1, waiting for transfers between devices, local(): lax.all_gather(feat_pad, 'ch', axis=0, tiled=True)  163 us
    scatter x2, local copies, waits for them, and re-layouts, pad_field(): padded.at[:, :, :, -1]  36.9 us
  transfers between devices with their start and end apart: 12, of which 7 were waited for; matrix products, arithmetic and copies ran while one was open for 2% of the time, Pallas kernels for 0%

commit v1 on v0

--- a/solution.py
+++ b/solution.py
@@ -72,7 +72,7 @@
         ],
         axis=2,
     )
-    return lax.psum(contrib.astype(jnp.bfloat16), ("px", "py"))
+    return jax.lax.psum(jax.lax.psum(contrib.astype(jnp.bfloat16), axis_name="px"), axis_name="py")
 
 
 def pad_field(field, edge_table, corner_table):

time: 1060 us -> 837 us (0.79)
  waiting for transfers between devices: 850 us -> 617 us
    psum x2 -> x4, waiting for transfers between devices: 521 us -> 289 us  [the longest x2 154 us: face_lines_of(): jax.lax.psum(contrib.astype(jnp.bfloat16), axis_name='px')]
  transfers between devices with their start and end apart: 12 -> 14, of which waited for: 7 -> 8; matrix products, arithmetic and copies ran while one was open for 2% -> 2% of each run, Pallas kernels for 0% -> 0%
where the time goes in v1:
time: 837 us; the launch traced here: 829 us
  waiting for transfers between devices  617 us (74%)
  local copies, waits for them, and re-layouts  119 us (14%)
  matrix products  36.3 us (4%)
  starting transfers between devices  27.3 us (3%)
  between operations  15.6 us (2%)
  other arithmetic  13.7 us (2%)
    all_gather x1, waiting for transfers between devices, local(): lax.all_gather(feat_pad, 'ch', axis=0, tiled=True)  162 us
    all_gather x1, waiting for transfers between devices, local(): lax.all_gather(grad_pad, 'ch', axis=0, tiled=True)  160 us
    psum x2, waiting for transfers between devices, face_lines_of(): jax.lax.psum(contrib.astype(jnp.bfloat16), axis_name='px')  154 us
    psum x2, waiting for transfers between devices, face_lines_of(): jax.lax.psum(jax.lax.psum(contrib.astype(jnp.bfloat16), axis_name='px'),...  135 us
    scatter x2, local copies, waits for them, and re-layouts, pad_field(): padded.at[:, :, :, -1]  36.9 us
    select_n x12, local copies, waits for them, and re-layouts, placed(): jnp.where(active, lax.dynamic_update_slice_in_dim(blank, values.astype(jn...  20.3 us
    dot_general x9, matrix products, forward_taps(): jnp.einsum('oc,cfab->ofab', taps[tap_row, tap_col], window, preferred_ele...  18.4 us
    dot_general x9, matrix products, backward_taps(): jnp.einsum('oc,ofab->cfab', taps[tap_row, tap_col], window, preferred_ele...  17.9 us
  transfers between devices with their start and end apart: 14, of which 8 were waited for; matrix products, arithmetic and copies ran while one was open for 2% of the time, Pallas kernels for 0%

profile of v1, /device:TPU:8, one launch (start us, length us, event | category | flops | bytes accessed | tf_op | source)
XLA Modules:
  0.0 828.6 jit_solution(11564096324096771008)
XLA Ops:
  11.2 3.0 copy.696
  16.0 2.7 select_n.196
  18.7 2.7 select_n.200
  23.0 2.6 copy.698
  27.0 7.1 collective-permute-start
  43.6 1.9 collective-permute-start.2
  45.5 3.6 collective-permute-start.3
  49.3 80.1 %all-reduce.5.cloned.1.call-done = bf16[16,12,4,128]{1,0,3,2:T(8,128)(2,1)} async-done(((bf16[16,12,4,128]{1,0,3,2:T(8,128)(2,1)}), bf16[16,12,4,128]{1,0,3,2:T(8,128)(2,1)}) %all-reduce.5.cloned.1.call-update) | async-done | bytes 196624 | tf_op jit(solution)/shard_map/psum | solution.py:75
  132.0 67.8 %all-reduce.7.cloned.1.call-done = bf16[16,12,4,128]{1,0,3,2:T(8,128)(2,1)} async-done(((bf16[16,12,4,128]{1,0,3,2:T(8,128)(2,1)}), bf16[16,12,4,128]{1,0,3,2:T(8,128)(2,1)}) %all-reduce.7.cloned.1.call-update) | async-done | bytes 196624 | tf_op jit(solution)/shard_map/psum | solution.py:75
  199.8 3.0 copy.702
  210.8 3.8 scatter.30
  218.6 18.3 %scatter.31 = bf16[16,12,18,34]{3,0,2,1:T(8,128)(2,1)S(1)} dynamic-update-slice(bf16[16,12,18,34]{3,0,2,1:T(8,128)(2,1)S(1)} %scatter.30, bf16[16,12,18,1]{3,0,2,1:T(8,128)(2,1)S(1)} %copy.707, s32[]{:T(128)} %constant.235.clone.1, s32[]{:T(128)} %constant.235.clone.1, s32[]{:T(128)} %constant.235.clone.1, s32[]{:T(128)} %constant.249.clone.1) | dynamic-update-slice | bytes 13828 | tf_op jit(solution)/shard_map/scatter | solution.py:97
  238.8 161.8 %all-gather.3.cloned.1.call-done = bf16[128,12,18,34]{3,0,2,1:T(8,128)(2,1)} async-done(((bf16[16,12,18,34]{3,0,2,1:T(8,128)(2,1)}), bf16[128,12,18,34]{3,0,2,1:T(8,128)(2,1)}) %all-gather.3.cloned.1.call-update) | async-done | bytes 1880080 | tf_op jit(solution)/shard_map/all_gather | solution.py:151
  400.6 4.7 fusion.20
  414.5 2.0 fusion.18
  416.5 2.6 fusion.37
  421.4 2.3 copy.725
  425.0 1.9 select_n.220
  427.0 1.9 select_n.223
  431.1 2.6 copy.727
  435.0 5.4 collective-permute-start.4
  444.3 5.7 collective-permute-done.5
  451.3 1.9 collective-permute-start.6
  453.3 3.6 collective-permute-start.7
  456.9 73.5 %all-reduce.9.cloned.1.call-done = bf16[16,12,4,128]{1,0,3,2:T(8,128)(2,1)} async-done(((bf16[16,12,4,128]{1,0,3,2:T(8,128)(2,1)}), bf16[16,12,4,128]{1,0,3,2:T(8,128)(2,1)}) %all-reduce.9.cloned.1.call-update) | async-done | bytes 196624 | tf_op jit(solution)/shard_map/psum | solution.py:75
  532.9 67.6 %all-reduce.11.cloned.1.call-done = bf16[16,12,4,128]{1,0,3,2:T(8,128)(2,1)} async-done(((bf16[16,12,4,128]{1,0,3,2:T(8,128)(2,1)}), bf16[16,12,4,128]{1,0,3,2:T(8,128)(2,1)}) %all-reduce.11.cloned.1.call-update) | async-done | bytes 196624 | tf_op jit(solution)/shard_map/psum | solution.py:75
  600.6 3.0 copy.731
  612.2 3.8 scatter.36
  619.4 18.6 %scatter.39 = bf16[16,12,18,34]{3,0,2,1:T(8,128)(2,1)S(1)} dynamic-update-slice(bf16[16,12,18,34]{3,0,2,1:T(8,128)(2,1)S(1)} %scatter.36, bf16[16,12,18,1]{3,0,2,1:T(8,128)(2,1)S(1)} %copy.735, s32[]{:T(128)} %constant.235.clone.1, s32[]{:T(128)} %constant.235.clone.1, s32[]{:T(128)} %constant.235.clone.1, s32[]{:T(128)} %constant.249.clone.1) | dynamic-update-slice | bytes 13828 | tf_op jit(solution)/shard_map/scatter | solution.py:97
  641.7 159.9 %all-gather.5.cloned.1.call-done = bf16[128,12,18,34]{3,0,2,1:T(8,128)(2,1)} async-done(((bf16[16,12,18,34]{3,0,2,1:T(8,128)(2,1)}), bf16[128,12,18,34]{3,0,2,1:T(8,128)(2,1)}) %all-gather.5.cloned.1.call-update) | async-done | bytes 1880080 | tf_op jit(solution)/shard_map/all_gather | solution.py:158
  801.6 4.8 fusion.2
  817.3 2.3 add_convert_fusion
  (203 shorter events, 86.3 us)
Async XLA Ops:
  7.2 393.5 %copy-start = (bf16[3,3,128,128]{3,2,1,0:T(8,128)(2,1)S(1)}, bf16[3,3,128,128]{3,2,1,0:T(8,128)(2,1)}, u32[]{:S(2)}) copy-start(bf16[3,3,128,128]{3,2,1,0:T(8,128)(2,1)} %param.27) | copy-start | bytes 884740
  7.2 122.2 %all-reduce.5.cloned.1.call-start = ((), (), s32[]{:S(2)}) async-start(), calls=%async_computation | async-start | bytes 4194304 | tf_op jit(solution)/shard_map/psum | solution.py:75
  25.7 10.9 %copy-start.15 = (s32[12,4,3]{0,1,2:T(4,128)S(1)}, s32[12,4,3]{0,1,2:T(4,128)}, u32[]{:S(2)}) copy-start(s32[12,4,3]{0,1,2:T(4,128)} %param.28) | copy-start | bytes 1732
  25.7 12.1 %copy-start.24 = (s32[12,4,2]{0,2,1:T(2,128)S(1)}, s32[12,4,2]{0,2,1:T(2,128)}, u32[]{:S(2)}) copy-start(s32[12,4,2]{0,2,1:T(2,128)} %param.29) | copy-start | bytes 1156
  25.7 174.1 %all-reduce.7.cloned.1.call-start = ((), (), s32[]{:S(2)}) async-start(), calls=%async_computation.1 | async-start | bytes 4194304 | tf_op jit(solution)/shard_map/psum | solution.py:75
  27.0 12.4 %collective-permute-start = (bf16[16,12,16,1]{2,0,3,1:T(8,128)(2,1)S(1)}, bf16[16,12,16,1]{2,0,3,1:T(8,128)(2,1)S(1)}, u32[]{:S(2)}, u32[]{:S(2)}) collective-permute-start(bf16[16,12,16,1]{2,0,3,1:T(8,128)(2,1)S(1)} %copy.684), channel_id=1, source_target_pairs={{0,64},{64,128},{128,192},{1,65},{65,129},{129,193},{2,66},{66,130... | collective-permute-start | bytes 18440 | tf_op jit(solution)/shard_map/ppermute | solution.py:16
  35.3 6.0 collective-permute-start.1
  43.6 86.1 %collective-permute-start.2 = (bf16[16,12,1,34]{3,0,1,2:T(8,128)(2,1)S(1)}, bf16[16,12,1,34]{3,0,1,2:T(8,128)(2,1)S(1)}, u32[]{:S(2)}, u32[]{:S(2)}) collective-permute-start(bf16[16,12,1,34]{3,0,1,2:T(8,128)(2,1)S(1)} %get-tuple-element.148), channel_id=1, source_target_pairs={{0,8},{8,16},{16,24},{24,32},{32,40},{40,48},{48,56},{1,9},{9,17},... | collective-permute-start | bytes 39176 | tf_op jit(solution)/shard_map/ppermute | solution.py:16
  45.5 84.2 %collective-permute-start.3 = (bf16[16,12,1,34]{3,0,1,2:T(8,128)(2,1)S(1)}, bf16[16,12,1,34]{3,0,1,2:T(8,128)(2,1)S(1)}, u32[]{:S(2)}, u32[]{:S(2)}) collective-permute-start(bf16[16,12,1,34]{3,0,1,2:T(8,128)(2,1)S(1)} %get-tuple-element.149), channel_id=1, source_target_pairs={{8,0},{16,8},{24,16},{32,24},{40,32},{48,40},{56,48},{9,1},{17,9},... | collective-permute-start | bytes 39176 | tf_op jit(solution)/shard_map/ppermute | solution.py:17
  129.4 271.2 %all-gather.3.cloned.1.call-start = ((), (), s32[]{:S(2)}) async-start(), calls=%async_computation.2 | async-start | bytes 7962624 | tf_op jit(solution)/shard_map/all_gather | solution.py:151
  131.9 71.8 %copy-start.13 = (pred[12]{0:T(512)(128)(4,1)S(1)}, pred[12]{0:T(512)(128)(4,1)}, u32[]{:S(2)}) copy-start(pred[12]{0:T(512)(128)(4,1)} %get-tuple-element.166) | copy-start | bytes 40
  131.9 72.6 %copy-start.11 = (pred[12]{0:T(512)(128)(4,1)S(1)}, pred[12]{0:T(512)(128)(4,1)}, u32[]{:S(2)}) copy-start(pred[12]{0:T(512)(128)(4,1)} %get-tuple-element.164) | copy-start | bytes 40
  131.9 75.5 %copy-start.18 = (pred[12]{0:T(512)(128)(4,1)S(1)}, pred[12]{0:T(512)(128)(4,1)}, u32[]{:S(2)}) copy-start(pred[12]{0:T(512)(128)(4,1)} %get-tuple-element.163) | copy-start | bytes 40
  202.8 4.7 copy-start.9
  202.8 4.8 copy-start.20
  204.7 4.5 copy-start.22
  217.3 21.1 %copy-start.5 = (bf16[16,12,1,1,512]{4,0,3,2,1:T(8,128)(2,1)S(1)}, bf16[16,12,1,1,512]{4,0,3,2,1:T(8,128)(2,1)}, u32[]{:S(2)}) copy-start(bf16[16,12,1,1,512]{4,0,3,2,1:T(8,128)(2,1)} %param.26) | copy-start | bytes 589828
  238.0 292.4 %all-reduce.9.cloned.1.call-start = ((), (), s32[]{:S(2)}) async-start(), calls=%async_computation.3 | async-start | bytes 4194304 | tf_op jit(solution)/shard_map/psum | solution.py:75
  400.6 4.8 copy-start.2
  433.7 166.8 %all-reduce.11.cloned.1.call-start = ((), (), s32[]{:S(2)}) async-start(), calls=%async_computation.4 | async-start | bytes 4194304 | tf_op jit(solution)/shard_map/psum | solution.py:75
  435.0 8.0 collective-permute-start.4
  441.7 8.3 collective-permute-start.5
  451.3 79.4 %collective-permute-start.6 = (bf16[16,12,1,34]{3,0,2,1:T(8,128)(2,1)S(1)}, bf16[16,12,1,34]{3,0,2,1:T(8,128)(2,1)S(1)}, u32[]{:S(2)}, u32[]{:S(2)}) collective-permute-start(bf16[16,12,1,34]{3,0,2,1:T(8,128)(2,1)S(1)} %get-tuple-element.128), channel_id=1, source_target_pairs={{0,8},{8,16},{16,24},{24,32},{32,40},{40,48},{48,56},{1,9},{9,17},... | collective-permute-start | bytes 39176 | tf_op jit(solution)/shard_map/ppermute | solution.py:16
  453.3 78.1 %collective-permute-start.7 = (bf16[16,12,1,34]{3,0,2,1:T(8,128)(2,1)S(1)}, bf16[16,12,1,34]{3,0,2,1:T(8,128)(2,1)}, u32[]{:S(2)}, u32[]{:S(2)}) collective-permute-start(bf16[16,12,1,34]{3,0,2,1:T(8,128)(2,1)S(1)} %get-tuple-element.129), channel_id=1, source_target_pairs={{8,0},{16,8},{24,16},{32,24},{40,32},{48,40},{56,48},{9,1},{17,9},... | collective-permute-start | bytes 39176 | tf_op jit(solution)/shard_map/ppermute | solution.py:17
  530.4 271.2 %all-gather.5.cloned.1.call-start = ((), (), s32[]{:S(2)}) async-start(), calls=%async_computation.5 | async-start | bytes 7962624 | tf_op jit(solution)/shard_map/all_gather | solution.py:158
  532.9 73.6 %copy-start.14 = (pred[12]{0:T(512)(128)(4,1)S(1)}, pred[12]{0:T(512)(128)(4,1)}, u32[]{:S(2)}) copy-start(pred[12]{0:T(512)(128)(4,1)} %get-tuple-element.166) | copy-start | bytes 40
  532.9 73.8 %copy-start.23 = (pred[12]{0:T(512)(128)(4,1)S(1)}, pred[12]{0:T(512)(128)(4,1)}, u32[]{:S(2)}) copy-start(pred[12]{0:T(512)(128)(4,1)} %get-tuple-element.162) | copy-start | bytes 40
  532.9 73.9 %copy-start.12 = (pred[12]{0:T(512)(128)(4,1)S(1)}, pred[12]{0:T(512)(128)(4,1)}, u32[]{:S(2)}) copy-start(pred[12]{0:T(512)(128)(4,1)} %get-tuple-element.164) | copy-start | bytes 40
  532.9 74.1 %copy-start.21 = (pred[12]{0:T(512)(128)(4,1)S(1)}, pred[12]{0:T(512)(128)(4,1)}, u32[]{:S(2)}) copy-start(pred[12]{0:T(512)(128)(4,1)} %get-tuple-element.161) | copy-start | bytes 40
  603.6 5.5 copy-start.19
  603.6 5.6 copy-start.7
  801.6 4.8 copy-start.1
  (7 other events, 8.1 us)
Sparse Core Ops, SparseCore 0:
  25.8 103.5 all-reduce.4
  131.9 67.8 all-reduce.6
  238.1 162.4 all-gather.2
  433.9 96.5 all-reduce.8
  532.6 67.8 all-reduce.10
  639.1 162.4 all-gather.4
